TPU v7x, 32 devices: a whole 2x2x4 slice. The times are simulated.
32 devices in a mesh: dp: 4 (over x, core), row: 2 (over y), col: 4 (over z).
Axes of the slice: x: 2, y: 2, z: 4, core: 2. Of those that a mesh axis runs over, the one named last changes fastest.
Arguments:
- tokens: bfloat16 [4096, 2048], P(('dp', 'row'), 'col'), may hold values from -6 to 6
- parent: int32 [4, 4], P('dp'), may hold values from -1 to 1, as said below
- depth: int32 [4, 4], P('dp'), may hold values from 0 to 2, as said below
- w_qkv: float32 [2048, 6144], P('row', 'col'), may hold values from -0.125 to 0.125
- b_qkv: float32 [6144], P('col'), may hold values from -3 to 3
- w_out: float32 [2048, 2048], P('col', 'row'), may hold values from -0.75 to 0.75
- w_up: float32 [2048, 8192], P('row', 'col'), may hold values from -0.125 to 0.125
- b_up: float32 [8192], P('col'), may hold values from -3 to 3
- w_down: float32 [8192, 2048], P('col', 'row'), may hold values from -0.0625 to 0.0625
- b_res: float32 [2048], P('col'), may hold values from -3 to 3
- ln_gain: float32 [2048], replicated, may hold values from 0.5 to 1.5
- ln_bias: float32 [2048], replicated, may hold values from -2 to 2
- cotangent: bfloat16 [4096, 2048], P(('dp', 'row'), 'col'), may hold values from -6 to 6
Outputs:
- output: bfloat16 [4096, 2048], P(('dp', 'row'), 'col')
- tokens_grad: float32 [4096, 2048], P(('dp', 'row'), 'col')
- w_qkv_grad: float32 [2048, 6144], P('row', 'col')
- b_qkv_grad: float32 [6144], P('col')
- w_out_grad: float32 [2048, 2048], P('col', 'row')
- w_up_grad: float32 [2048, 8192], P('row', 'col')
- b_up_grad: float32 [8192], P('col')
- w_down_grad: float32 [8192, 2048], P('col', 'row')
- b_res_grad: float32 [2048], P('col')
- ln_gain_grad: float32 [2048], replicated
- ln_bias_grad: float32 [2048], replicated
Inputs may be any that keep to these rules, and one draw needn't show every extreme that they name: In every tree segments 0 to 1 form a trunk: segment 0 has parent -1 and each other trunk segment j has parent j - 1. Every later segment has a trunk segment as parent, and the last segment's parent is trunk segment 4 // 2 - 1. Segment 0 has depth 0 and every other segment one more than its parent.
All inputs are finite; a program needn't handle non-finite values.
Results may differ from a plain program's by a relative error of at most 0.018.
Values may be sent and summed in bfloat16 or wider, within the bound.
No kernel may reach another device: no remote copies, remote signals or barrier semaphores. Data moves between devices by JAX's collectives and lax.ppermute only.
A program may use at most 256 MiB of HBM per device.

v0:
```python
import functools
import math
import jax
import jax.numpy as jnp
from jax import lax
from jax.sharding import PartitionSpec as P

HD = 64
ROT = 32
SEG = 256
norm_epsilon = 1e-05
masked_fill = -1e30
rotary_base = 10000.0


def precise_dot(left, right):
    return jnp.dot(left, right, precision=lax.Precision.HIGHEST, preferred_element_type=jnp.float32)


def ancestry(parent_row):
    seg_count = parent_row.shape[0]
    labels = jnp.arange(seg_count, dtype=jnp.int32)
    identity = jnp.eye(seg_count, dtype=jnp.float32)
    parent_hot = (parent_row[:, None] == labels[None, :]).astype(jnp.float32)

    def extend(rounds, reachable):
        return jnp.minimum(identity + precise_dot(parent_hot, reachable), 1.0)

    return lax.fori_loop(0, seg_count, extend, identity)


def rotate(values, cosines, sines):
    half_rot = ROT // 2
    former = values[..., :half_rot]
    latter = values[..., half_rot:ROT]
    return jnp.concatenate(
        [former * cosines - latter * sines, latter * cosines + former * sines, values[..., ROT:]],
        axis=-1,
    )


def angles_of(positions):
    frequency = jnp.exp(
        -math.log(rotary_base) * 2.0 * jnp.arange(ROT // 2, dtype=jnp.float32) / ROT
    )
    phase_angle = positions[:, None] * frequency[None, :]
    return (jnp.cos(phase_angle)[:, None, :], jnp.sin(phase_angle)[:, None, :])


def reorder_rows(gradient, row_count, dp_count):
    leading = gradient.shape[0]
    blocked = gradient.reshape(
        row_count, dp_count, leading // (row_count * dp_count), gradient.shape[1]
    )
    return jnp.transpose(blocked, (1, 0, 2, 3)).reshape(leading, gradient.shape[1])


def reorder_cols(gradient, row_count, dp_count):
    trailing = gradient.shape[1]
    blocked = gradient.reshape(
        gradient.shape[0], row_count, dp_count, trailing // (row_count * dp_count)
    )
    return jnp.transpose(blocked, (0, 2, 1, 3)).reshape(gradient.shape[0], trailing)


def per_device(
    tokens,
    parent,
    depth,
    w_qkv,
    b_qkv,
    w_out,
    w_up,
    b_up,
    w_down,
    b_res,
    ln_gain,
    ln_bias,
    cotangent,
):
    tok_rows = tokens.shape[0]
    col_width = tokens.shape[1]
    row_count = lax.axis_size("row")
    dp_count = lax.axis_size("dp")
    row_start = lax.axis_index("row") * tok_rows
    local_heads = w_out.shape[0] // HD
    seg_count = parent.shape[1]
    labels = jnp.arange(seg_count, dtype=jnp.int32)
    reachable = ancestry(parent[0])
    query_index = row_start + jnp.arange(tok_rows, dtype=jnp.int32)
    query_seg = query_index // SEG
    query_hot = (query_seg[:, None] == labels[None, :]).astype(jnp.float32)
    query_reach = precise_dot(query_hot, reachable)
    levels = precise_dot(query_hot, depth[0].astype(jnp.float32)[:, None])[:, 0]
    positions = levels * SEG + (query_index % SEG).astype(jnp.float32)
    cosines, sines = angles_of(positions)
    score_scale = HD ** (-0.5)

    def permit(key_len):
        key_index = jnp.arange(key_len, dtype=jnp.int32)
        key_seg = key_index // SEG
        key_hot = (key_seg[:, None] == labels[None, :]).astype(jnp.float32)
        linked = precise_dot(query_reach, key_hot.T) > 0.5
        return linked & (
            (query_seg[:, None] != key_seg[None, :]) | (query_index[:, None] >= key_index[None, :])
        )

    whole = lax.all_gather(tokens, "col", axis=1, tiled=True).astype(jnp.float32)
    centred = whole - jnp.mean(whole, axis=1, keepdims=True)
    inv_scale = lax.rsqrt(jnp.mean(centred * centred, axis=1, keepdims=True) + norm_epsilon)
    normal = centred * inv_scale
    normed = (normal * ln_gain + ln_bias).astype(jnp.bfloat16)
    qkv_full, up_full, out_full, down_full = (
        lax.all_gather(w_qkv.astype(jnp.bfloat16), "row", axis=0, tiled=True),
        lax.all_gather(w_up.astype(jnp.bfloat16), "row", axis=0, tiled=True),
        lax.all_gather(w_out.astype(jnp.bfloat16), "row", axis=1, tiled=True),
        lax.all_gather(w_down.astype(jnp.bfloat16), "row", axis=1, tiled=True),
    )
    mixed = (jnp.dot(normed, qkv_full, preferred_element_type=jnp.float32) + b_qkv).reshape(
        tok_rows, local_heads, 3, HD
    )

    def rotate_pair(query_pre, key_pre):
        return (rotate(query_pre, cosines, sines), rotate(key_pre, cosines, sines))

    rotated, rotate_back = jax.vjp(rotate_pair, mixed[:, :, 0], mixed[:, :, 1])
    queries = rotated[0].astype(jnp.bfloat16)
    key_rows = rotated[1].astype(jnp.bfloat16)
    value_rows = mixed[:, :, 2].astype(jnp.bfloat16)
    key_flat = key_rows.reshape(tok_rows, local_heads * HD)
    value_flat = value_rows.reshape(tok_rows, local_heads * HD)

    def scores_for(key_part):
        raw_scores = (
            jnp.einsum("qhe,khe->hqk", queries, key_part, preferred_element_type=jnp.float32)
            * score_scale
        )
        allowed = permit(key_part.shape[0])
        return (jnp.where(allowed[None], raw_scores, masked_fill), allowed)

    pieces = (
        lax.all_gather(key_flat, "row", axis=0, tiled=True),
        lax.all_gather(value_flat, "row", axis=0, tiled=True),
    )
    running_top = jnp.full((local_heads, tok_rows), masked_fill, jnp.float32)
    key_len = pieces[0].shape[0]
    key_part = pieces[0].reshape(key_len, local_heads, HD)
    value_part = pieces[1].reshape(key_len, local_heads, HD)
    scores, allowed = scores_for(key_part)
    new_top = jnp.maximum(running_top, jnp.max(scores, axis=2))
    exponent = jnp.where(allowed[None], jnp.exp(scores - new_top[:, :, None]), 0.0)
    running_sum = jnp.sum(exponent, axis=2)
    weighted = jnp.einsum(
        "hqk,khe->hqe",
        exponent.astype(jnp.bfloat16),
        value_part,
        preferred_element_type=jnp.float32,
    )
    running_top, running_sum, weighted = (new_top, running_sum, weighted)
    log_total = running_top + jnp.log(running_sum)
    attn_exact = weighted / running_sum[:, :, None]
    attended = (
        jnp.transpose(attn_exact, (1, 0, 2))
        .reshape(tok_rows, local_heads * HD)
        .astype(jnp.bfloat16)
    )
    hidden_up = jnp.dot(normed, up_full, preferred_element_type=jnp.float32) + b_up
    activated, gelu_back = jax.vjp(functools.partial(jax.nn.gelu, approximate=True), hidden_up)
    activated = activated.astype(jnp.bfloat16)
    branch_terms = jnp.dot(attended, out_full, preferred_element_type=jnp.float32) + jnp.dot(
        activated, down_full, preferred_element_type=jnp.float32
    )
    branch = lax.psum_scatter(
        branch_terms.astype(jnp.bfloat16), "col", scatter_dimension=1, tiled=True
    ).astype(jnp.float32)
    output = (tokens.astype(jnp.float32) + branch + b_res).astype(jnp.bfloat16)
    grad_full = lax.all_gather(cotangent, "col", axis=1, tiled=True)
    res_bias_grad = jnp.sum(cotangent.astype(jnp.float32), axis=0)
    down_grad = jnp.einsum("tf,td->fd", activated, grad_full, preferred_element_type=jnp.float32)
    out_grad = jnp.einsum("te,td->ed", attended, grad_full, preferred_element_type=jnp.float32)
    act_grad = jnp.einsum("td,fd->tf", grad_full, down_full, preferred_element_type=jnp.float32)
    up_grad = gelu_back(act_grad)[0].astype(jnp.bfloat16)
    attn_grad = jnp.einsum(
        "td,ed->te", grad_full, out_full, preferred_element_type=jnp.float32
    ).astype(jnp.bfloat16)
    up_bias_grad = jnp.sum(up_grad.astype(jnp.float32), axis=0)
    up_weight_grad = jnp.einsum("td,tf->df", normed, up_grad, preferred_element_type=jnp.float32)
    out_heads = attn_grad.reshape(tok_rows, local_heads, HD)
    delta_sum = jnp.einsum("qhe,hqe->hq", out_heads.astype(jnp.float32), attn_exact)
    pieces = (
        lax.all_gather(key_flat, "row", axis=0, tiled=True),
        lax.all_gather(value_flat, "row", axis=0, tiled=True),
    )
    key_len = pieces[0].shape[0]
    key_part = pieces[0].reshape(key_len, local_heads, HD)
    value_part = pieces[1].reshape(key_len, local_heads, HD)
    scores, allowed = scores_for(key_part)
    softmaxed = jnp.where(allowed[None], jnp.exp(scores - log_total[:, :, None]), 0.0)
    prob_grad = jnp.einsum(
        "qhe,khe->hqk", out_heads, value_part, preferred_element_type=jnp.float32
    )
    score_grad = (softmaxed * (prob_grad - delta_sum[:, :, None])).astype(jnp.bfloat16)
    query_grad = (
        jnp.einsum("hqk,khe->qhe", score_grad, key_part, preferred_element_type=jnp.float32)
        * score_scale
    )
    key_grad = (
        jnp.einsum("hqk,qhe->khe", score_grad, queries, preferred_element_type=jnp.float32)
        * score_scale
    )
    value_grad = jnp.einsum(
        "hqk,qhe->khe",
        softmaxed.astype(jnp.bfloat16),
        out_heads,
        preferred_element_type=jnp.float32,
    )
    stacked = jnp.stack([key_grad, value_grad], axis=1).reshape(key_len, 2 * local_heads * HD)
    pair_grad = stacked
    query_grad, pair_grad = (query_grad, pair_grad)
    own_pairs = (
        lax.psum_scatter(pair_grad.astype(jnp.bfloat16), "row", scatter_dimension=0, tiled=True)
        .astype(jnp.float32)
        .reshape(tok_rows, 2, local_heads, HD)
    )
    query_pre, key_pre = rotate_back((query_grad, own_pairs[:, 0]))
    mixed_grad = (
        jnp.stack([query_pre, key_pre, own_pairs[:, 1]], axis=2)
        .reshape(tok_rows, 3 * local_heads * HD)
        .astype(jnp.bfloat16)
    )
    qkv_bias_grad = jnp.sum(mixed_grad.astype(jnp.float32), axis=0)
    qkv_weight_grad = jnp.einsum(
        "td,tc->dc", normed, mixed_grad, preferred_element_type=jnp.float32
    )
    norm_part = jnp.einsum(
        "tc,dc->td", mixed_grad, qkv_full, preferred_element_type=jnp.float32
    ) + jnp.einsum("tf,df->td", up_grad, up_full, preferred_element_type=jnp.float32)
    norm_grad = lax.psum(norm_part.astype(jnp.bfloat16), "col").astype(jnp.float32)
    gain_grad = jnp.sum(norm_grad * normal, axis=0)
    shift_grad = jnp.sum(norm_grad, axis=0)
    scaled = norm_grad * ln_gain
    mean_scaled = jnp.mean(scaled, axis=1, keepdims=True)
    mean_mixed = jnp.mean(scaled * normal, axis=1, keepdims=True)
    col_start = lax.axis_index("col") * col_width
    scaled_share = lax.dynamic_slice_in_dim(scaled, col_start, col_width, 1)
    normal_share = lax.dynamic_slice_in_dim(normal, col_start, col_width, 1)
    tokens_grad = inv_scale * (
        scaled_share - mean_scaled - normal_share * mean_mixed
    ) + cotangent.astype(jnp.float32)
    qkv_bias_grad, up_bias_grad, res_bias_grad, gain_grad, shift_grad = (
        lax.psum(qkv_bias_grad.astype(jnp.bfloat16), ("dp", "row")).astype(jnp.float32),
        lax.psum(up_bias_grad.astype(jnp.bfloat16), ("dp", "row")).astype(jnp.float32),
        lax.psum(res_bias_grad.astype(jnp.bfloat16), ("dp", "row")).astype(jnp.float32),
        lax.psum(gain_grad.astype(jnp.bfloat16), ("dp", "row")).astype(jnp.float32),
        lax.psum(shift_grad.astype(jnp.bfloat16), ("dp", "row")).astype(jnp.float32),
    )
    pieces_now = (
        lax.psum_scatter(
            reorder_rows(qkv_weight_grad, row_count, dp_count).astype(jnp.bfloat16),
            ("dp", "row"),
            scatter_dimension=0,
            tiled=True,
        ).astype(jnp.float32),
        lax.psum_scatter(
            reorder_rows(up_weight_grad, row_count, dp_count).astype(jnp.bfloat16),
            ("dp", "row"),
            scatter_dimension=0,
            tiled=True,
        ).astype(jnp.float32),
        lax.psum_scatter(
            reorder_cols(out_grad, row_count, dp_count).astype(jnp.bfloat16),
            ("dp", "row"),
            scatter_dimension=1,
            tiled=True,
        ).astype(jnp.float32),
        lax.psum_scatter(
            reorder_cols(down_grad, row_count, dp_count).astype(jnp.bfloat16),
            ("dp", "row"),
            scatter_dimension=1,
            tiled=True,
        ).astype(jnp.float32),
    )
    qkv_weight_grad, up_weight_grad, out_grad, down_grad = (
        lax.all_gather(pieces_now[0].astype(jnp.bfloat16), "dp", axis=0, tiled=True).astype(
            jnp.float32
        ),
        lax.all_gather(pieces_now[1].astype(jnp.bfloat16), "dp", axis=0, tiled=True).astype(
            jnp.float32
        ),
        lax.all_gather(pieces_now[2].astype(jnp.bfloat16), "dp", axis=1, tiled=True).astype(
            jnp.float32
        ),
        lax.all_gather(pieces_now[3].astype(jnp.bfloat16), "dp", axis=1, tiled=True).astype(
            jnp.float32
        ),
    )
    return (
        output,
        tokens_grad,
        qkv_weight_grad,
        qkv_bias_grad,
        out_grad,
        up_weight_grad,
        up_bias_grad,
        down_grad,
        res_bias_grad,
        gain_grad,
        shift_grad,
    )


def solution(mesh):
    return jax.shard_map(
        per_device,
        mesh=mesh,
        in_specs=(
            P(("dp", "row"), "col"),
            P("dp", None),
            P("dp", None),
            P("row", "col"),
            P("col"),
            P("col", "row"),
            P("row", "col"),
            P("col"),
            P("col", "row"),
            P("col"),
            P(),
            P(),
            P(("dp", "row"), "col"),
        ),
        out_specs=(
            P(("dp", "row"), "col"),
            P(("dp", "row"), "col"),
            P("row", "col"),
            P("col"),
            P("col", "row"),
            P("row", "col"),
            P("col"),
            P("col", "row"),
            P("col"),
            P(),
            P(),
        ),
        check_vma=False,
    )
```

profile of v0, /device:TPU:0, one launch (start us, length us, event | category | flops | bytes accessed | tf_op | source)
XLA Modules:
  0.0 1054.9 jit_solution(18216092555689512656)
XLA Ops:
  8.0 5.0 convert_element_type.211
  16.1 41.9 %all-gather.13.cloned.1.call-done = bf16[512,2048]{1,0:T(8,128)(2,1)} async-done(((bf16[512,512]{1,0:T(8,128)(2,1)}), bf16[512,2048]{1,0:T(8,128)(2,1)}) %all-gather.13.cloned.1.call-update) | async-done | bytes 2097168 | tf_op jit(solution)/shard_map/all_gather | solution.py:108
  62.4 76.9 %all-gather.15.cloned.1.call-done = bf16[2048,1536]{1,0:T(8,128)(2,1)} async-done(((bf16[1024,1536]{1,0:T(8,128)(2,1)}), bf16[2048,1536]{1,0:T(8,128)(2,1)}) %all-gather.15.cloned.1.call-update) | async-done | bytes 6291472 | tf_op jit(solution)/shard_map/all_gather | solution.py:114
  139.3 7.9 convolution_add_fusion.1
  153.1 6.1 convert_element_type.221
  159.3 6.1 convert_element_type.223
  168.9 5.6 all-gather.21.cloned.1.call-done
  174.5 47.1 %all-gather.27.cloned.1.call-done = bf16[512,2048]{1,0:T(8,128)(2,1)} async-done(((bf16[512,512]{1,0:T(8,128)(2,1)}), bf16[512,2048]{1,0:T(8,128)(2,1)}) %all-gather.27.cloned.1.call-update) | async-done | bytes 2097168 | tf_op jit(solution)/shard_map/all_gather | solution.py:177
  221.6 4.3 convolution_convert_fusion.2
  227.0 16.7 %all-gather.17.cloned.1.call-done = bf16[1024,512]{0,1:T(8,128)(2,1)} async-done(((bf16[512,512]{0,1:T(8,128)(2,1)}), bf16[1024,512]{0,1:T(8,128)(2,1)}) %all-gather.17.cloned.1.call-update) | async-done | bytes 1048592 | tf_op jit(solution)/shard_map/all_gather | solution.py:142
  243.7 4.4 fusion.68
  248.2 4.3 fusion.7
  254.9 12.1 %all-gather.19.cloned.1.call-done = bf16[1024,512]{0,1:T(8,128)(2,1)} async-done(((bf16[512,512]{0,1:T(8,128)(2,1)}), bf16[1024,512]{0,1:T(8,128)(2,1)}) %all-gather.19.cloned.1.call-update) | async-done | bytes 1048592 | tf_op jit(solution)/shard_map/all_gather | solution.py:143
  267.0 8.6 fusion.41
  276.5 3.6 copy-done.1
  280.0 9.9 multiply_convert_fusion
  289.9 5.1 fusion.38
  295.0 3.6 fusion.35
  300.2 6.5 fusion.39
  307.6 65.6 %all-gather.23.cloned.1.call-done = bf16[2048,2048]{1,0:T(8,128)(2,1)} async-done(((bf16[1024,2048]{1,0:T(8,128)(2,1)}), bf16[2048,2048]{1,0:T(8,128)(2,1)}) %all-gather.23.cloned.1.call-update) | async-done | bytes 8388624 | tf_op jit(solution)/shard_map/all_gather | solution.py:115
  373.2 9.9 fusion.64
  383.0 96.3 %all-gather.25.cloned.1.call-done = bf16[2048,2048]{1,0:T(8,128)(2,1)} async-done(((bf16[2048,1024]{1,0:T(8,128)(2,1)}), bf16[2048,2048]{1,0:T(8,128)(2,1)}) %all-gather.25.cloned.1.call-update) | async-done | bytes 8388624 | tf_op jit(solution)/shard_map/all_gather | solution.py:117
  479.3 13.4 %fusion.65 = (bf16[2048]{0:T(1024)(128)(2,1)S(1)}, bf16[512,2048]{1,0:T(8,128)(2,1)}) fusion(f32[512,2048]{1,0:T(8,128)} %fusion.64, f32[2048]{0:T(1024)S(1)} %copy-done.29, bf16[512,2048]{1,0:T(8,128)(2,1)} %all-gather.27.cloned.1.call-done, bf16[2048,2048]{1,0:T(8,128)(2,1)} %all-gather.25.cloned.1.call-done), kind=kOutput, calls=%fused_computation.132 | convolution fusion | flops 4318033920 | bytes 16789504 | tf_op jit(solution)/shard_map/td,fd->tf/dot_general | solution.py:181
  492.7 21.3 %reduce-scatter.9.cloned.1.call-done = bf16[512,1024]{0,1:T(8,128)(2,1)} async-done(((bf16[1024,1024]{0,1:T(8,128)(2,1)}), bf16[512,1024]{0,1:T(8,128)(2,1)}) %reduce-scatter.9.cloned.1.call-update) | async-done | bytes 1048592 | tf_op jit(solution)/shard_map/reduce_scatter | solution.py:221
  519.3 3.5 fusion.69
  522.8 7.6 add_convert_fusion
  530.5 4.0 copy.53
  539.1 8.8 convolution_convert_fusion.1
  547.8 8.5 copy.56
  556.4 11.0 %convolution_convert_fusion = bf16[2048,2048]{0,1:T(8,128)(2,1)} fusion(bf16[512,2048]{1,0:T(8,128)(2,1)} %all-gather.27.cloned.1.call-done, f32[512,2048]{1,0:T(8,128)} %fusion.64, f32[2048]{0:T(1024)S(1)} %copy-done.29), kind=kOutput, calls=%fused_computation.21 | convolution fusion | flops 4309647360 | bytes 14688256 | tf_op jit(solution)/shard_map/tf,td->fd/dot_general | solution.py:179
  567.4 21.7 %copy.57 = bf16[2048,4,2,256]{3,2,1,0:T(2,128)(2,1)} copy(bf16[2048,4,2,256]{0,3,1,2:T(8,128)(2,1)} %bitcast.110) | data formatting | bytes 16777216 | tf_op jit(solution)/shard_map/convert_element_type | solution.py:277
  589.2 14.4 %convert_element_type.255 = bf16[2048,2048]{1,0:T(8,128)(2,1)} reshape(bf16[2048,4,2,256]{3,2,1,0:T(2,128)(2,1)} %copy.57) | data formatting | bytes 16777216 | tf_op jit(solution)/shard_map/convert_element_type | solution.py:277
  603.7 13.1 %all-reduce.9.cloned.1.call-done = bf16[512,2048]{1,0:T(8,128)(2,1)} async-done(((bf16[512,2048]{1,0:T(8,128)(2,1)}), bf16[512,2048]{1,0:T(8,128)(2,1)}) %all-reduce.9.cloned.1.call-update) | async-done | bytes 2097168 | tf_op jit(solution)/shard_map/psum | solution.py:238
  616.7 6.3 fusion.21
  625.9 5.2 convert_bitcast_fusion
  634.6 25.6 %reduce-scatter.13.cloned.1.call-done = bf16[512,256]{0,1:T(8,128)(2,1)} async-done(((bf16[512,2048]{0,1:T(8,128)(2,1)}), bf16[512,256]{0,1:T(8,128)(2,1)}) %reduce-scatter.13.cloned.1.call-update) | async-done | bytes 262160 | tf_op jit(solution)/shard_map/reduce_scatter | solution.py:270
  660.3 9.3 fusion.62
  672.4 63.2 %reduce-scatter.15.cloned.1.call-done = bf16[256,2048]{1,0:T(8,128)(2,1)} async-done(((bf16[2048,2048]{1,0:T(8,128)(2,1)}), bf16[256,2048]{1,0:T(8,128)(2,1)}) %reduce-scatter.15.cloned.1.call-update) | async-done | bytes 1048592 | tf_op jit(solution)/shard_map/reduce_scatter | solution.py:264
  735.7 75.3 %reduce-scatter.17.cloned.1.call-done = bf16[2048,256]{1,0:T(8,128)(2,1)} async-done(((bf16[2048,2048]{1,0:T(8,128)(2,1)}), bf16[2048,256]{1,0:T(8,128)(2,1)}) %reduce-scatter.17.cloned.1.call-update) | async-done | bytes 1048592 | tf_op jit(solution)/shard_map/reduce_scatter | solution.py:276
  811.1 65.6 %reduce-scatter.11.cloned.1.call-done = bf16[256,1536]{1,0:T(8,128)(2,1)} async-done(((bf16[2048,1536]{1,0:T(8,128)(2,1)}), bf16[256,1536]{1,0:T(8,128)(2,1)}) %reduce-scatter.11.cloned.1.call-update) | async-done | bytes 786448 | tf_op jit(solution)/shard_map/reduce_scatter | solution.py:258
  876.9 17.9 %all-gather.31.cloned.1.call-done = bf16[512,1024]{0,1:T(8,128)(2,1)} async-done(((bf16[512,256]{0,1:T(8,128)(2,1)}), bf16[512,1024]{0,1:T(8,128)(2,1)}) %all-gather.31.cloned.1.call-update) | async-done | bytes 1048592 | tf_op jit(solution)/shard_map/all_gather | solution.py:290
  897.3 43.2 %reduce-scatter.7.cloned.1.call-done = bf16[512,512]{1,0:T(8,128)(2,1)} async-done(((bf16[512,2048]{1,0:T(8,128)(2,1)}), bf16[512,512]{1,0:T(8,128)(2,1)}) %reduce-scatter.7.cloned.1.call-update) | async-done | bytes 524304 | tf_op jit(solution)/shard_map/reduce_scatter | solution.py:173
  942.9 25.2 %all-reduce.6 = (bf16[1536]{0:T(1024)(128)(2,1)S(1)}, bf16[2048]{0:T(1024)(128)(2,1)S(1)}, bf16[512]{0:T(512)(128)(2,1)S(1)}, bf16[2048]{0:T(1024)(128)(2,1)S(1)}, bf16[2048]{0:T(1024)(128)(2,1)S(1)}) all-reduce(bf16[1536]{0:T(1024)(128)(2,1)S(1)} %reduce_sum.110, ...), channel_id=1, replica_groups=mesh['dp'=4,'row'=2,'col'=4] {'dp','row'}, use_global_device_ids=true, to_apply=%region_13.14 | all-reduce | flops 8192 | bytes 32768 | tf_op jit(solution)/shard_map/psum | solution.py:251
  975.8 6.7 convert_element_type.250
  982.5 29.9 %all-gather.35.cloned.1.call-done = bf16[2048,1024]{1,0:T(8,128)(2,1)} async-done(((bf16[2048,256]{1,0:T(8,128)(2,1)}), bf16[2048,1024]{1,0:T(8,128)(2,1)}) %all-gather.35.cloned.1.call-update) | async-done | bytes 4194320 | tf_op jit(solution)/shard_map/all_gather | solution.py:293
  1012.3 6.6 convert_element_type.256
  1019.0 23.5 %all-gather.29.cloned.1.call-done = bf16[1024,1536]{1,0:T(8,128)(2,1)} async-done(((bf16[256,1536]{1,0:T(8,128)(2,1)}), bf16[1024,1536]{1,0:T(8,128)(2,1)}) %all-gather.29.cloned.1.call-update) | async-done | bytes 3145744 | tf_op jit(solution)/shard_map/all_gather | solution.py:284
  1042.4 5.5 convert_element_type.240
  (175 shorter events, 57.2 us)
Async XLA Ops:
  7.2 50.8 %all-gather.13.cloned.1.call-start = ((), (), s32[]{:S(2)}) async-start(), calls=%async_computation.6 | async-start | bytes 2621440 | tf_op jit(solution)/shard_map/all_gather | solution.py:108
  7.9 5.1 copy-start.7
  7.9 131.4 %all-gather.15.cloned.1.call-start = ((), (), s32[]{:S(2)}) async-start(), calls=%async_computation.7 | async-start | bytes 9437184 | tf_op jit(solution)/shard_map/all_gather | solution.py:114
  13.0 126.3 %copy-start.23 = (f32[2048]{0:T(1024)S(1)}, f32[2048]{0:T(1024)}, u32[]{:S(2)}) copy-start(f32[2048]{0:T(1024)} %param.26) | copy-start | bytes 24580
  13.0 126.3 %copy-start.25 = (f32[2048]{0:T(1024)S(1)}, f32[2048]{0:T(1024)}, u32[]{:S(2)}) copy-start(f32[2048]{0:T(1024)} %param.25) | copy-start | bytes 24580
  13.0 126.3 %copy-start.28 = (f32[1536]{0:T(1024)S(1)}, f32[1536]{0:T(1024)}, u32[]{:S(2)}) copy-start(f32[1536]{0:T(1024)} %param.19) | copy-start | bytes 18436
  13.0 161.5 %all-gather.21.cloned.1.call-start = ((), (), s32[]{:S(2)}) async-start(), calls=%async_computation.10 | async-start | bytes 3145728 | tf_op jit(solution)/shard_map/all_gather | solution.py:116
  14.2 207.4 %all-gather.27.cloned.1.call-start = ((), (), s32[]{:S(2)}) async-start(), calls=%async_computation.14 | async-start | bytes 2621440 | tf_op jit(solution)/shard_map/all_gather | solution.py:177
  14.8 228.9 %all-gather.17.cloned.1.call-start = ((), (), s32[]{:S(2)}) async-start(), calls=%async_computation.8 | async-start | bytes 1572864 | tf_op jit(solution)/shard_map/all_gather | solution.py:142
  58.0 81.3 %copy-start.2 = (bf16[512,2048]{1,0:T(8,128)(2,1)S(1)}, bf16[512,2048]{1,0:T(8,128)(2,1)}, u32[]{:S(2)}) copy-start(bf16[512,2048]{1,0:T(8,128)(2,1)} %all-gather.13.cloned.1.call-done) | copy-start | bytes 6291460
  152.2 114.9 %all-gather.19.cloned.1.call-start = ((), (), s32[]{:S(2)}) async-start(), calls=%async_computation.9 | async-start | bytes 1572864 | tf_op jit(solution)/shard_map/all_gather | solution.py:143
  153.1 220.1 %all-gather.23.cloned.1.call-start = ((), (), s32[]{:S(2)}) async-start(), calls=%async_computation.11 | async-start | bytes 12582912 | tf_op jit(solution)/shard_map/all_gather | solution.py:115
  159.2 320.1 %all-gather.25.cloned.1.call-start = ((), (), s32[]{:S(2)}) async-start(), calls=%async_computation.12 | async-start | bytes 12582912 | tf_op jit(solution)/shard_map/all_gather | solution.py:117
  165.4 348.7 %reduce-scatter.9.cloned.1.call-start = ((), (), s32[]{:S(2)}) async-start(), calls=%async_computation.15 | async-start | bytes 3145728 | tf_op jit(solution)/shard_map/reduce_scatter | solution.py:221
  248.2 6.1 copy-start
  248.2 6.1 copy-start.21
  254.3 12.7 %copy-start.19 = (f32[8,512]{1,0:T(8,128)}, f32[8,512]{1,0:T(8,128)S(1)}, u32[]{:S(2)}) copy-start(f32[8,512]{1,0:T(8,128)S(1)} %fusion.7) | copy-start | bytes 49156
  267.0 8.6 copy-start.13
  267.0 8.6 copy-start.20
  267.0 13.0 %copy-start.1 = (f32[8,512,1024]{2,1,0:T(8,128)S(1)}, f32[8,512,1024]{2,1,0:T(8,128)}, u32[]{:S(2)}) copy-start(f32[8,512,1024]{2,1,0:T(8,128)} %copy-done) | copy-start | bytes 50331652
  289.9 5.1 copy-start.14
  289.9 5.1 copy-start.22
  300.1 73.0 %copy-start.3 = (bf16[512,2048]{1,0:T(8,128)(2,1)S(1)}, bf16[512,2048]{1,0:T(8,128)(2,1)}, u32[]{:S(2)}) copy-start(bf16[512,2048]{1,0:T(8,128)(2,1)} %all-gather.13.cloned.1.call-done) | copy-start | bytes 6291460
  300.2 73.0 %copy-start.24 = (f32[2048]{0:T(1024)S(1)}, f32[2048]{0:T(1024)}, u32[]{:S(2)}) copy-start(f32[2048]{0:T(1024)} %param.26) | copy-start | bytes 24580
  300.2 73.0 %copy-start.26 = (f32[2048]{0:T(1024)S(1)}, f32[2048]{0:T(1024)}, u32[]{:S(2)}) copy-start(f32[2048]{0:T(1024)} %param.25) | copy-start | bytes 24580
  300.2 316.6 %all-reduce.9.cloned.1.call-start = ((), (), s32[]{:S(2)}) async-start(), calls=%async_computation.16 | async-start | bytes 4194304 | tf_op jit(solution)/shard_map/psum | solution.py:238
  307.6 171.7 %copy-start.29 = (f32[2048]{0:T(1024)S(1)}, f32[2048]{0:T(1024)}, u32[]{:S(2)}) copy-start(f32[2048]{0:T(1024)} %param.22) | copy-start | bytes 24580
  492.7 23.0 %copy-start.16 = (f32[512,16]{0,1:T(8,128)S(1)}, f32[512,16]{0,1:T(8,128)}, u32[]{:S(2)}) copy-start(f32[512,16]{0,1:T(8,128)} %get-tuple-element.101) | copy-start | bytes 98308
  492.7 23.0 %copy-start.18 = (f32[512,16]{0,1:T(8,128)S(1)}, f32[512,16]{0,1:T(8,128)}, u32[]{:S(2)}) copy-start(f32[512,16]{0,1:T(8,128)} %get-tuple-element.102) | copy-start | bytes 98308
  516.1 3.2 slice-start.3
  516.5 6.2 slice-start
  516.7 6.1 copy-start.11
  519.3 3.5 slice-start.1
  530.4 4.0 copy-start.12
  530.4 129.8 %reduce-scatter.13.cloned.1.call-start = ((), (), s32[]{:S(2)}) async-start(), calls=%async_computation.19 | async-start | bytes 2359296 | tf_op jit(solution)/shard_map/reduce_scatter | solution.py:270
  539.0 196.6 %reduce-scatter.15.cloned.1.call-start = ((), (), s32[]{:S(2)}) async-start(), calls=%async_computation.21 | async-start | bytes 9437184 | tf_op jit(solution)/shard_map/reduce_scatter | solution.py:264
  556.4 254.6 %reduce-scatter.17.cloned.1.call-start = ((), (), s32[]{:S(2)}) async-start(), calls=%async_computation.23 | async-start | bytes 9437184 | tf_op jit(solution)/shard_map/reduce_scatter | solution.py:276
  603.6 273.0 %reduce-scatter.11.cloned.1.call-start = ((), (), s32[]{:S(2)}) async-start(), calls=%async_computation.17 | async-start | bytes 7077888 | tf_op jit(solution)/shard_map/reduce_scatter | solution.py:258
  634.5 260.2 %all-gather.31.cloned.1.call-start = ((), (), s32[]{:S(2)}) async-start(), calls=%async_computation.20 | async-start | bytes 1310720 | tf_op jit(solution)/shard_map/all_gather | solution.py:290
  660.2 9.3 copy-start.10
  660.2 280.3 %reduce-scatter.7.cloned.1.call-start = ((), (), s32[]{:S(2)}) async-start(), calls=%async_computation.13 | async-start | bytes 2621440 | tf_op jit(solution)/shard_map/reduce_scatter | solution.py:173
  672.3 204.3 %copy-start.5 = (bf16[512,512]{1,0:T(8,128)(2,1)S(1)}, bf16[512,512]{1,0:T(8,128)(2,1)}, u32[]{:S(2)}) copy-start(bf16[512,512]{1,0:T(8,128)(2,1)} %param.27) | copy-start | bytes 1572868
  672.3 268.2 %copy-start.8 = (bf16[512,512]{1,0:T(8,128)(2,1)S(1)}, bf16[512,512]{1,0:T(8,128)(2,1)}, u32[]{:S(2)}) copy-start(bf16[512,512]{1,0:T(8,128)(2,1)} %param.15) | copy-start | bytes 1572868
  672.3 268.2 %copy-start.27 = (f32[512]{0:T(512)S(1)}, f32[512]{0:T(512)}, u32[]{:S(2)}) copy-start(f32[512]{0:T(512)} %param.24) | copy-start | bytes 6148
  672.3 270.2 %copy-start.4 = (bf16[512,2048]{1,0:T(8,128)(2,1)S(1)}, bf16[512,2048]{1,0:T(8,128)(2,1)}, u32[]{:S(2)}) copy-start(bf16[512,2048]{1,0:T(8,128)(2,1)} %all-reduce.9.cloned.1.call-done) | copy-start | bytes 6291460
  672.4 303.5 %all-gather.33.cloned.1.call-start = ((), (), s32[]{:S(2)}) async-start(), calls=%async_computation.22 | async-start | bytes 5242880 | tf_op jit(solution)/shard_map/all_gather | solution.py:287
  735.6 276.7 %all-gather.35.cloned.1.call-start = ((), (), s32[]{:S(2)}) async-start(), calls=%async_computation.24 | async-start | bytes 5242880 | tf_op jit(solution)/shard_map/all_gather | solution.py:293
  811.0 231.4 %all-gather.29.cloned.1.call-start = ((), (), s32[]{:S(2)}) async-start(), calls=%async_computation.18 | async-start | bytes 3932160 | tf_op jit(solution)/shard_map/all_gather | solution.py:284
  (7 other events, 10.7 us)
Sparse Core Ops, SparseCore 0:
  9.6 48.3 all-gather.12
  60.1 79.1 all-gather.14
  141.4 33.0 all-gather.20
  176.0 45.6 all-gather.26
  223.6 20.0 all-gather.16
  245.7 21.2 all-gather.18
  269.1 104.0 all-gather.22
  375.3 103.9 all-gather.24
  482.1 31.8 reduce-scatter.8
  530.5 86.1 all-reduce.8
  620.0 40.1 reduce-scatter.12
  664.1 71.4 reduce-scatter.14
  739.7 71.2 reduce-scatter.16
  814.8 61.7 reduce-scatter.10
  878.0 16.6 all-gather.30
  896.9 43.6 reduce-scatter.6
  942.0 33.8 all-gather.32
  977.2 35.0 all-gather.34
  1013.9 28.4 all-gather.28
where the time goes:
time: 1060 us; the launch traced here: 1050 us
  waiting for transfers between devices  744 us (70%)
  matrix products  128 us (12%)
  local copies, waits for them, and re-layouts  74.6 us (7%)
  other arithmetic  67.1 us (6%)
  blocking collectives  25.2 us (2%)
  between operations  15 us (1%)
    all_gather x1, waiting for transfers between devices, per_device(): lax.all_gather(w_down.astype(jnp.bfloat16), 'row', axis=1, tiled=True)  96.3 us
    all_gather x1, waiting for transfers between devices, per_device(): lax.all_gather(w_qkv.astype(jnp.bfloat16), 'row', axis=0, tiled=True)  76.9 us
    reduce_scatter x1, waiting for transfers between devices, per_device(): lax.psum_scatter(reorder_cols(down_grad, row_count, dp_count).astype(jnp....  75.3 us
    all_gather x1, waiting for transfers between devices, per_device(): lax.all_gather(w_up.astype(jnp.bfloat16), 'row', axis=0, tiled=True)  65.6 us
    reduce_scatter x1, waiting for transfers between devices, per_device(): lax.psum_scatter(reorder_rows(qkv_weight_grad, row_count, dp_count).astyp...  65.6 us
    reduce_scatter x1, waiting for transfers between devices, per_device(): lax.psum_scatter(reorder_rows(up_weight_grad, row_count, dp_count).astype...  63.2 us
    all_gather x1, waiting for transfers between devices, per_device(): grad_full = lax.all_gather(cotangent, 'col', axis=1, tiled=True)  47.1 us
    reduce_scatter x1, waiting for transfers between devices, per_device(): lax.psum_scatter(branch_terms.astype(jnp.bfloat16), 'col', scatter_dimens...  43.2 us
  transfers between devices with their start and end apart: 19, of which 19 were waited for; matrix products, arithmetic and copies ran while one was open for 23% of the time, Pallas kernels for 0%

commit v1 on v0

--- a/solution.py
+++ b/solution.py
@@ -248,7 +248,9 @@
         scaled_share - mean_scaled - normal_share * mean_mixed
     ) + cotangent.astype(jnp.float32)
     qkv_bias_grad, up_bias_grad, res_bias_grad, gain_grad, shift_grad = (
-        lax.psum(qkv_bias_grad.astype(jnp.bfloat16), ("dp", "row")).astype(jnp.float32),
+        jax.lax.all_gather(qkv_bias_grad.astype(jnp.bfloat16), ("dp", "row"))
+        .sum(axis=0)
+        .astype(jnp.float32),
         lax.psum(up_bias_grad.astype(jnp.bfloat16), ("dp", "row")).astype(jnp.float32),
         lax.psum(res_bias_grad.astype(jnp.bfloat16), ("dp", "row")).astype(jnp.float32),
         lax.psum(gain_grad.astype(jnp.bfloat16), ("dp", "row")).astype(jnp.float32),

time: 1060 us -> 1060 us (level)
  blocking collectives: 25.2 us -> 40 us
  waiting for transfers between devices: 744 us -> 730 us
    all_gather x1, waiting for transfers between devices: 17.9 us -> 2.64 us  [per_device(): lax.all_gather(pieces_now[2].astype(jnp.bfloat16), 'dp', axis=1, tiled=True)]
    all_gather x0 -> x1, blocking collectives: none -> 14.8 us  [per_device(): jax.lax.all_gather(qkv_bias_grad.astype(jnp.bfloat16), ('dp', 'row'))]
where the time goes in v1:
time: 1060 us
  waiting for transfers between devices  730 us (69%)
  matrix products  128 us (12%)
  local copies, waits for them, and re-layouts  74.6 us (7%)
  other arithmetic  67.2 us (6%)
  blocking collectives  40 us (4%)
  between operations  15 us (1%)
    all_gather x1, waiting for transfers between devices, per_device(): lax.all_gather(w_down.astype(jnp.bfloat16), 'row', axis=1, tiled=True)  96.3 us
    all_gather x1, waiting for transfers between devices, per_device(): lax.all_gather(w_qkv.astype(jnp.bfloat16), 'row', axis=0, tiled=True)  76.9 us
    reduce_scatter x1, waiting for transfers between devices, per_device(): lax.psum_scatter(reorder_cols(down_grad, row_count, dp_count).astype(jnp....  75.3 us
    all_gather x1, waiting for transfers between devices, per_device(): lax.all_gather(w_up.astype(jnp.bfloat16), 'row', axis=0, tiled=True)  65.6 us
    reduce_scatter x1, waiting for transfers between devices, per_device(): lax.psum_scatter(reorder_rows(qkv_weight_grad, row_count, dp_count).astyp...  65.5 us
    reduce_scatter x1, waiting for transfers between devices, per_device(): lax.psum_scatter(reorder_rows(up_weight_grad, row_count, dp_count).astype...  63.2 us
    all_gather x1, waiting for transfers between devices, per_device(): grad_full = lax.all_gather(cotangent, 'col', axis=1, tiled=True)  47.1 us
    reduce_scatter x1, waiting for transfers between devices, per_device(): lax.psum_scatter(branch_terms.astype(jnp.bfloat16), 'col', scatter_dimens...  43.2 us
  transfers between devices with their start and end apart: 19, of which 19 were waited for; matrix products, arithmetic and copies ran while one was open for 23% of the time, Pallas kernels for 0%

profile of v1, /device:TPU:0, one launch (start us, length us, event | category | flops | bytes accessed | tf_op | source)
XLA Modules:
  0.0 1055.1 jit_solution(9910991833248770281)
XLA Ops:
  8.0 5.0 convert_element_type.213
  16.1 41.9 %all-gather.14.cloned.1.call-done = bf16[512,2048]{1,0:T(8,128)(2,1)} async-done(((bf16[512,512]{1,0:T(8,128)(2,1)}), bf16[512,2048]{1,0:T(8,128)(2,1)}) %all-gather.14.cloned.1.call-update) | async-done | bytes 2097168 | tf_op jit(solution)/shard_map/all_gather | solution.py:108
  62.4 76.9 %all-gather.16.cloned.1.call-done = bf16[2048,1536]{1,0:T(8,128)(2,1)} async-done(((bf16[1024,1536]{1,0:T(8,128)(2,1)}), bf16[2048,1536]{1,0:T(8,128)(2,1)}) %all-gather.16.cloned.1.call-update) | async-done | bytes 6291472 | tf_op jit(solution)/shard_map/all_gather | solution.py:114
  139.3 7.9 convolution_add_fusion.1
  153.1 6.1 convert_element_type.223
  159.3 6.1 convert_element_type.225
  168.9 5.6 all-gather.22.cloned.1.call-done
  174.5 47.1 %all-gather.28.cloned.1.call-done = bf16[512,2048]{1,0:T(8,128)(2,1)} async-done(((bf16[512,512]{1,0:T(8,128)(2,1)}), bf16[512,2048]{1,0:T(8,128)(2,1)}) %all-gather.28.cloned.1.call-update) | async-done | bytes 2097168 | tf_op jit(solution)/shard_map/all_gather | solution.py:177
  221.6 4.3 convolution_convert_fusion.2
  227.0 16.7 %all-gather.18.cloned.1.call-done = bf16[1024,512]{0,1:T(8,128)(2,1)} async-done(((bf16[512,512]{0,1:T(8,128)(2,1)}), bf16[1024,512]{0,1:T(8,128)(2,1)}) %all-gather.18.cloned.1.call-update) | async-done | bytes 1048592 | tf_op jit(solution)/shard_map/all_gather | solution.py:142
  243.7 4.4 fusion.68
  248.2 4.3 fusion.7
  254.9 12.1 %all-gather.20.cloned.1.call-done = bf16[1024,512]{0,1:T(8,128)(2,1)} async-done(((bf16[512,512]{0,1:T(8,128)(2,1)}), bf16[1024,512]{0,1:T(8,128)(2,1)}) %all-gather.20.cloned.1.call-update) | async-done | bytes 1048592 | tf_op jit(solution)/shard_map/all_gather | solution.py:143
  267.0 8.6 fusion.41
  276.5 3.6 copy-done.1
  280.0 9.9 multiply_convert_fusion
  289.9 5.1 fusion.38
  295.0 3.6 fusion.35
  300.2 6.5 fusion.39
  307.6 65.6 %all-gather.24.cloned.1.call-done = bf16[2048,2048]{1,0:T(8,128)(2,1)} async-done(((bf16[1024,2048]{1,0:T(8,128)(2,1)}), bf16[2048,2048]{1,0:T(8,128)(2,1)}) %all-gather.24.cloned.1.call-update) | async-done | bytes 8388624 | tf_op jit(solution)/shard_map/all_gather | solution.py:115
  373.2 9.8 fusion.64
  383.0 96.3 %all-gather.26.cloned.1.call-done = bf16[2048,2048]{1,0:T(8,128)(2,1)} async-done(((bf16[2048,1024]{1,0:T(8,128)(2,1)}), bf16[2048,2048]{1,0:T(8,128)(2,1)}) %all-gather.26.cloned.1.call-update) | async-done | bytes 8388624 | tf_op jit(solution)/shard_map/all_gather | solution.py:117
  479.3 13.4 %fusion.65 = (bf16[2048]{0:T(1024)(128)(2,1)S(1)}, bf16[512,2048]{1,0:T(8,128)(2,1)}) fusion(f32[512,2048]{1,0:T(8,128)} %fusion.64, f32[2048]{0:T(1024)S(1)} %copy-done.29, bf16[512,2048]{1,0:T(8,128)(2,1)} %all-gather.28.cloned.1.call-done, bf16[2048,2048]{1,0:T(8,128)(2,1)} %all-gather.26.cloned.1.call-done), kind=kOutput, calls=%fused_computation.132 | convolution fusion | flops 4318033920 | bytes 16789504 | tf_op jit(solution)/shard_map/td,fd->tf/dot_general | solution.py:181
  492.7 21.3 %reduce-scatter.9.cloned.1.call-done = bf16[512,1024]{0,1:T(8,128)(2,1)} async-done(((bf16[1024,1024]{0,1:T(8,128)(2,1)}), bf16[512,1024]{0,1:T(8,128)(2,1)}) %reduce-scatter.9.cloned.1.call-update) | async-done | bytes 1048592 | tf_op jit(solution)/shard_map/reduce_scatter | solution.py:221
  519.3 3.5 fusion.69
  522.8 7.6 add_convert_fusion
  530.5 4.0 copy.53
  539.1 8.8 convolution_convert_fusion.1
  547.8 8.5 copy.56
  556.4 11.0 %convolution_convert_fusion = bf16[2048,2048]{0,1:T(8,128)(2,1)} fusion(bf16[512,2048]{1,0:T(8,128)(2,1)} %all-gather.28.cloned.1.call-done, f32[512,2048]{1,0:T(8,128)} %fusion.64, f32[2048]{0:T(1024)S(1)} %copy-done.29), kind=kOutput, calls=%fused_computation.21 | convolution fusion | flops 4309647360 | bytes 14688256 | tf_op jit(solution)/shard_map/tf,td->fd/dot_general | solution.py:179
  567.4 21.7 %copy.57 = bf16[2048,4,2,256]{3,2,1,0:T(2,128)(2,1)} copy(bf16[2048,4,2,256]{0,3,1,2:T(8,128)(2,1)} %bitcast.110) | data formatting | bytes 16777216 | tf_op jit(solution)/shard_map/convert_element_type | solution.py:279
  589.2 14.4 %convert_element_type.257 = bf16[2048,2048]{1,0:T(8,128)(2,1)} reshape(bf16[2048,4,2,256]{3,2,1,0:T(2,128)(2,1)} %copy.57) | data formatting | bytes 16777216 | tf_op jit(solution)/shard_map/convert_element_type | solution.py:279
  603.7 13.0 %all-reduce.9.cloned.1.call-done = bf16[512,2048]{1,0:T(8,128)(2,1)} async-done(((bf16[512,2048]{1,0:T(8,128)(2,1)}), bf16[512,2048]{1,0:T(8,128)(2,1)}) %all-reduce.9.cloned.1.call-update) | async-done | bytes 2097168 | tf_op jit(solution)/shard_map/psum | solution.py:238
  616.7 6.3 fusion.21
  625.9 5.2 convert_bitcast_fusion
  634.6 25.6 %reduce-scatter.13.cloned.1.call-done = bf16[512,256]{0,1:T(8,128)(2,1)} async-done(((bf16[512,2048]{0,1:T(8,128)(2,1)}), bf16[512,256]{0,1:T(8,128)(2,1)}) %reduce-scatter.13.cloned.1.call-update) | async-done | bytes 262160 | tf_op jit(solution)/shard_map/reduce_scatter | solution.py:272
  660.3 9.3 fusion.62
  672.4 63.2 %reduce-scatter.15.cloned.1.call-done = bf16[256,2048]{1,0:T(8,128)(2,1)} async-done(((bf16[2048,2048]{1,0:T(8,128)(2,1)}), bf16[256,2048]{1,0:T(8,128)(2,1)}) %reduce-scatter.15.cloned.1.call-update) | async-done | bytes 1048592 | tf_op jit(solution)/shard_map/reduce_scatter | solution.py:266
  735.7 75.3 %reduce-scatter.17.cloned.1.call-done = bf16[2048,256]{1,0:T(8,128)(2,1)} async-done(((bf16[2048,2048]{1,0:T(8,128)(2,1)}), bf16[2048,256]{1,0:T(8,128)(2,1)}) %reduce-scatter.17.cloned.1.call-update) | async-done | bytes 1048592 | tf_op jit(solution)/shard_map/reduce_scatter | solution.py:278
  811.1 65.5 %reduce-scatter.11.cloned.1.call-done = bf16[256,1536]{1,0:T(8,128)(2,1)} async-done(((bf16[2048,1536]{1,0:T(8,128)(2,1)}), bf16[256,1536]{1,0:T(8,128)(2,1)}) %reduce-scatter.11.cloned.1.call-update) | async-done | bytes 786448 | tf_op jit(solution)/shard_map/reduce_scatter | solution.py:260
  876.8 14.8 %all-gather = bf16[8,1,1536]{2,1,0:T(2,128)(2,1)S(1)} all-gather(bf16[1,1,1536]{2,1,0:T(2,128)(2,1)S(1)} %reshape.249), channel_id=1, replica_groups=mesh['dp'=4,'row'=2,'col'=4] {'dp','row'}, dimensions={0}, use_global_device_ids=true | all-gather | bytes 27648 | tf_op jit(solution)/shard_map/all_gather | solution.py:251
  897.5 43.2 %reduce-scatter.7.cloned.1.call-done = bf16[512,512]{1,0:T(8,128)(2,1)} async-done(((bf16[512,2048]{1,0:T(8,128)(2,1)}), bf16[512,512]{1,0:T(8,128)(2,1)}) %reduce-scatter.7.cloned.1.call-update) | async-done | bytes 524304 | tf_op jit(solution)/shard_map/reduce_scatter | solution.py:173
  943.1 25.2 %all-reduce.6 = (bf16[2048]{0:T(1024)(128)(2,1)S(1)}, bf16[512]{0:T(512)(128)(2,1)S(1)}, bf16[2048]{0:T(1024)(128)(2,1)S(1)}, bf16[2048]{0:T(1024)(128)(2,1)S(1)}) all-reduce(bf16[2048]{0:T(1024)(128)(2,1)S(1)} %get-tuple-element.79, bf16[512]{0:T(512)(128)(2,1)S(1)} %reduce_sum.122, ...), channel_id=1, replica_groups=mesh['dp'=4,'row'=2,'col'=4] {'dp','row'}, use_global_device_ids=true, to_apply=%region_17.18 | all-reduce | flops 6656 | bytes 26624 | tf_op jit(solution)/shard_map/psum | solution.py:254
  976.0 6.7 convert_element_type.252
  982.7 29.9 %all-gather.36.cloned.1.call-done = bf16[2048,1024]{1,0:T(8,128)(2,1)} async-done(((bf16[2048,256]{1,0:T(8,128)(2,1)}), bf16[2048,1024]{1,0:T(8,128)(2,1)}) %all-gather.36.cloned.1.call-update) | async-done | bytes 4194320 | tf_op jit(solution)/shard_map/all_gather | solution.py:295
  1012.5 6.6 convert_element_type.258
  1019.1 23.5 %all-gather.30.cloned.1.call-done = bf16[1024,1536]{1,0:T(8,128)(2,1)} async-done(((bf16[256,1536]{1,0:T(8,128)(2,1)}), bf16[1024,1536]{1,0:T(8,128)(2,1)}) %all-gather.30.cloned.1.call-update) | async-done | bytes 3145744 | tf_op jit(solution)/shard_map/all_gather | solution.py:286
  1042.6 5.5 convert_element_type.242
  (177 shorter events, 60.5 us)
Async XLA Ops:
  7.2 50.8 %all-gather.14.cloned.1.call-start = ((), (), s32[]{:S(2)}) async-start(), calls=%async_computation.6 | async-start | bytes 2621440 | tf_op jit(solution)/shard_map/all_gather | solution.py:108
  7.9 5.1 copy-start.7
  7.9 131.4 %all-gather.16.cloned.1.call-start = ((), (), s32[]{:S(2)}) async-start(), calls=%async_computation.7 | async-start | bytes 9437184 | tf_op jit(solution)/shard_map/all_gather | solution.py:114
  13.0 126.3 %copy-start.23 = (f32[2048]{0:T(1024)S(1)}, f32[2048]{0:T(1024)}, u32[]{:S(2)}) copy-start(f32[2048]{0:T(1024)} %param.26) | copy-start | bytes 24580
  13.0 126.3 %copy-start.25 = (f32[2048]{0:T(1024)S(1)}, f32[2048]{0:T(1024)}, u32[]{:S(2)}) copy-start(f32[2048]{0:T(1024)} %param.25) | copy-start | bytes 24580
  13.0 126.3 %copy-start.28 = (f32[1536]{0:T(1024)S(1)}, f32[1536]{0:T(1024)}, u32[]{:S(2)}) copy-start(f32[1536]{0:T(1024)} %param.19) | copy-start | bytes 18436
  13.0 161.5 %all-gather.22.cloned.1.call-start = ((), (), s32[]{:S(2)}) async-start(), calls=%async_computation.10 | async-start | bytes 3145728 | tf_op jit(solution)/shard_map/all_gather | solution.py:116
  14.2 207.4 %all-gather.28.cloned.1.call-start = ((), (), s32[]{:S(2)}) async-start(), calls=%async_computation.14 | async-start | bytes 2621440 | tf_op jit(solution)/shard_map/all_gather | solution.py:177
  14.8 228.9 %all-gather.18.cloned.1.call-start = ((), (), s32[]{:S(2)}) async-start(), calls=%async_computation.8 | async-start | bytes 1572864 | tf_op jit(solution)/shard_map/all_gather | solution.py:142
  58.0 81.3 %copy-start.2 = (bf16[512,2048]{1,0:T(8,128)(2,1)S(1)}, bf16[512,2048]{1,0:T(8,128)(2,1)}, u32[]{:S(2)}) copy-start(bf16[512,2048]{1,0:T(8,128)(2,1)} %all-gather.14.cloned.1.call-done) | copy-start | bytes 6291460
  152.2 114.9 %all-gather.20.cloned.1.call-start = ((), (), s32[]{:S(2)}) async-start(), calls=%async_computation.9 | async-start | bytes 1572864 | tf_op jit(solution)/shard_map/all_gather | solution.py:143
  153.1 220.1 %all-gather.24.cloned.1.call-start = ((), (), s32[]{:S(2)}) async-start(), calls=%async_computation.11 | async-start | bytes 12582912 | tf_op jit(solution)/shard_map/all_gather | solution.py:115
  159.2 320.1 %all-gather.26.cloned.1.call-start = ((), (), s32[]{:S(2)}) async-start(), calls=%async_computation.12 | async-start | bytes 12582912 | tf_op jit(solution)/shard_map/all_gather | solution.py:117
  165.4 348.7 %reduce-scatter.9.cloned.1.call-start = ((), (), s32[]{:S(2)}) async-start(), calls=%async_computation.15 | async-start | bytes 3145728 | tf_op jit(solution)/shard_map/reduce_scatter | solution.py:221
  248.2 6.1 copy-start
  248.2 6.1 copy-start.21
  254.3 12.7 %copy-start.19 = (f32[8,512]{1,0:T(8,128)}, f32[8,512]{1,0:T(8,128)S(1)}, u32[]{:S(2)}) copy-start(f32[8,512]{1,0:T(8,128)S(1)} %fusion.7) | copy-start | bytes 49156
  267.0 8.6 copy-start.13
  267.0 8.6 copy-start.20
  267.0 13.0 %copy-start.1 = (f32[8,512,1024]{2,1,0:T(8,128)S(1)}, f32[8,512,1024]{2,1,0:T(8,128)}, u32[]{:S(2)}) copy-start(f32[8,512,1024]{2,1,0:T(8,128)} %copy-done) | copy-start | bytes 50331652
  289.9 5.1 copy-start.14
  289.9 5.1 copy-start.22
  300.1 73.0 %copy-start.3 = (bf16[512,2048]{1,0:T(8,128)(2,1)S(1)}, bf16[512,2048]{1,0:T(8,128)(2,1)}, u32[]{:S(2)}) copy-start(bf16[512,2048]{1,0:T(8,128)(2,1)} %all-gather.14.cloned.1.call-done) | copy-start | bytes 6291460
  300.2 73.0 %copy-start.24 = (f32[2048]{0:T(1024)S(1)}, f32[2048]{0:T(1024)}, u32[]{:S(2)}) copy-start(f32[2048]{0:T(1024)} %param.26) | copy-start | bytes 24580
  300.2 73.0 %copy-start.26 = (f32[2048]{0:T(1024)S(1)}, f32[2048]{0:T(1024)}, u32[]{:S(2)}) copy-start(f32[2048]{0:T(1024)} %param.25) | copy-start | bytes 24580
  300.2 316.5 %all-reduce.9.cloned.1.call-start = ((), (), s32[]{:S(2)}) async-start(), calls=%async_computation.16 | async-start | bytes 4194304 | tf_op jit(solution)/shard_map/psum | solution.py:238
  307.6 171.7 %copy-start.29 = (f32[2048]{0:T(1024)S(1)}, f32[2048]{0:T(1024)}, u32[]{:S(2)}) copy-start(f32[2048]{0:T(1024)} %param.22) | copy-start | bytes 24580
  492.7 23.0 %copy-start.16 = (f32[512,16]{0,1:T(8,128)S(1)}, f32[512,16]{0,1:T(8,128)}, u32[]{:S(2)}) copy-start(f32[512,16]{0,1:T(8,128)} %get-tuple-element.100) | copy-start | bytes 98308
  492.7 23.0 %copy-start.18 = (f32[512,16]{0,1:T(8,128)S(1)}, f32[512,16]{0,1:T(8,128)}, u32[]{:S(2)}) copy-start(f32[512,16]{0,1:T(8,128)} %get-tuple-element.101) | copy-start | bytes 98308
  516.1 3.2 slice-start.3
  516.5 6.2 slice-start
  516.7 6.1 copy-start.11
  519.3 3.5 slice-start.1
  530.4 4.0 copy-start.12
  530.4 129.8 %reduce-scatter.13.cloned.1.call-start = ((), (), s32[]{:S(2)}) async-start(), calls=%async_computation.19 | async-start | bytes 2359296 | tf_op jit(solution)/shard_map/reduce_scatter | solution.py:272
  539.0 196.6 %reduce-scatter.15.cloned.1.call-start = ((), (), s32[]{:S(2)}) async-start(), calls=%async_computation.21 | async-start | bytes 9437184 | tf_op jit(solution)/shard_map/reduce_scatter | solution.py:266
  556.4 254.6 %reduce-scatter.17.cloned.1.call-start = ((), (), s32[]{:S(2)}) async-start(), calls=%async_computation.23 | async-start | bytes 9437184 | tf_op jit(solution)/shard_map/reduce_scatter | solution.py:278
  603.6 272.9 %reduce-scatter.11.cloned.1.call-start = ((), (), s32[]{:S(2)}) async-start(), calls=%async_computation.17 | async-start | bytes 7077888 | tf_op jit(solution)/shard_map/reduce_scatter | solution.py:260
  634.5 260.4 %all-gather.32.cloned.1.call-start = ((), (), s32[]{:S(2)}) async-start(), calls=%async_computation.20 | async-start | bytes 1310720 | tf_op jit(solution)/shard_map/all_gather | solution.py:292
  660.2 9.3 copy-start.10
  660.2 280.5 %reduce-scatter.7.cloned.1.call-start = ((), (), s32[]{:S(2)}) async-start(), calls=%async_computation.13 | async-start | bytes 2621440 | tf_op jit(solution)/shard_map/reduce_scatter | solution.py:173
  672.3 204.3 %copy-start.5 = (bf16[512,512]{1,0:T(8,128)(2,1)S(1)}, bf16[512,512]{1,0:T(8,128)(2,1)}, u32[]{:S(2)}) copy-start(bf16[512,512]{1,0:T(8,128)(2,1)} %param.27) | copy-start | bytes 1572868
  672.3 268.5 %copy-start.8 = (bf16[512,512]{1,0:T(8,128)(2,1)S(1)}, bf16[512,512]{1,0:T(8,128)(2,1)}, u32[]{:S(2)}) copy-start(bf16[512,512]{1,0:T(8,128)(2,1)} %param.15) | copy-start | bytes 1572868
  672.3 268.5 %copy-start.27 = (f32[512]{0:T(512)S(1)}, f32[512]{0:T(512)}, u32[]{:S(2)}) copy-start(f32[512]{0:T(512)} %param.24) | copy-start | bytes 6148
  672.3 270.4 %copy-start.4 = (bf16[512,2048]{1,0:T(8,128)(2,1)S(1)}, bf16[512,2048]{1,0:T(8,128)(2,1)}, u32[]{:S(2)}) copy-start(bf16[512,2048]{1,0:T(8,128)(2,1)} %all-reduce.9.cloned.1.call-done) | copy-start | bytes 6291460
  672.3 303.7 %all-gather.34.cloned.1.call-start = ((), (), s32[]{:S(2)}) async-start(), calls=%async_computation.22 | async-start | bytes 5242880 | tf_op jit(solution)/shard_map/all_gather | solution.py:289
  735.6 276.9 %all-gather.36.cloned.1.call-start = ((), (), s32[]{:S(2)}) async-start(), calls=%async_computation.24 | async-start | bytes 5242880 | tf_op jit(solution)/shard_map/all_gather | solution.py:295
  811.0 231.6 %all-gather.30.cloned.1.call-start = ((), (), s32[]{:S(2)}) async-start(), calls=%async_computation.18 | async-start | bytes 3932160 | tf_op jit(solution)/shard_map/all_gather | solution.py:286
  (7 other events, 10.7 us)
Sparse Core Ops, SparseCore 0:
  9.6 48.3 all-gather.13
  60.1 79.1 all-gather.15
  141.4 33.0 all-gather.21
  176.0 45.6 all-gather.27
  223.6 20.0 all-gather.17
  245.7 21.2 all-gather.19
  269.1 104.0 all-gather.23
  375.3 103.9 all-gather.25
  482.1 31.8 reduce-scatter.8
  530.5 86.1 all-reduce.8
  620.0 40.1 reduce-scatter.12
  664.1 71.5 reduce-scatter.14
  739.6 71.2 reduce-scatter.16
  814.8 61.7 reduce-scatter.10
  878.0 16.8 all-gather.31
  897.1 43.6 reduce-scatter.6
  942.2 33.8 all-gather.33
  977.4 35.0 all-gather.35
  1014.1 28.4 all-gather.29
